TPU v7x, 128 devices: a whole 4x4x4 slice. The times are simulated.
128 devices in a mesh: rows: 8 (over y, core), acts: 16 (over z, x).
Axes of the slice: x: 4, y: 4, z: 4, core: 2. Of those that a mesh axis runs over, the one named last changes fastest.
Arguments:
- features: bfloat16 [32768, 2048], P('rows'), may hold values from -6 to 80
- policy_weight: bfloat16 [2048, 4096], P(None, 'acts'), may hold values from -3 to 3
- reward_weight: bfloat16 [2048, 4096], P(None, 'acts'), may hold values from -1 to 1
- logged_action: int32 [32768], P('rows'), may hold values from 0 to 4095
- reward_level: int32 [32768], P('rows'), may hold values from 0 to 4
- logged_propensity: float32 [32768], P('rows'), may hold values from 9.765625e-05 to 0.0009765625
Outputs:
- policy_grad: float32 [2048, 4096], P(None, 'acts')
- reward_grad: float32 [2048, 4096], P(None, 'acts')
- row_value: float32 [32768], P('rows')
All inputs are finite; a program needn't handle non-finite values.
Results may differ from a plain program's by a relative error of at most 0.015.
Values may be sent and summed in bfloat16 or wider, within the bound.
No kernel may reach another device: no remote copies, remote signals or barrier semaphores. Data moves between devices by JAX's collectives and lax.ppermute only.
A program may use at most 128 MiB of HBM per device.

v0:
```python
import jax
import jax.numpy as jnp
from jax import lax
from jax.sharding import PartitionSpec as P


def finish_rows(
    exponent, row_total, weighted, picked_exp, picked_pred, predicted, onehot, payoff, propensity
):
    probability = exponent / row_total[:, None]
    mean_pred = weighted / row_total
    importance = picked_exp / row_total / propensity
    corrected = importance * (payoff - picked_pred)
    row_value = mean_pred + corrected
    policy_term = (
        probability * (predicted - mean_pred[:, None])
        + corrected[:, None] * (onehot.astype(jnp.float32) - probability)
    ).astype(jnp.bfloat16)
    reward_term = jnp.where(onehot, predicted - payoff[:, None], jnp.float32(0.0)).astype(
        jnp.bfloat16
    )
    return (policy_term, reward_term, row_value)


def on_device(
    features, policy_weight, reward_weight, logged_action, reward_level, logged_propensity
):
    scores = jnp.dot(features, policy_weight, preferred_element_type=jnp.float32)
    predicted = jnp.dot(features, reward_weight, preferred_element_type=jnp.float32)
    act_block = scores.shape[1]
    payoff = reward_level.astype(jnp.float32) * 0.25
    full_scores, full_pred = (
        lax.all_to_all(scores, "acts", split_axis=0, concat_axis=1, tiled=True),
        lax.all_to_all(predicted, "acts", split_axis=0, concat_axis=1, tiled=True),
    )
    part_rows = full_scores.shape[0]
    offset = lax.axis_index("acts") * part_rows
    my_action = lax.dynamic_slice_in_dim(logged_action, offset, part_rows)
    my_payoff = lax.dynamic_slice_in_dim(payoff, offset, part_rows)
    my_propensity = lax.dynamic_slice_in_dim(logged_propensity, offset, part_rows)
    all_columns = jnp.arange(full_scores.shape[1], dtype=jnp.int32)
    row_onehot = my_action[:, None] == all_columns[None, :]
    largest = jnp.max(full_scores, axis=1, keepdims=True)
    exponent = jnp.exp(full_scores - largest)
    row_total = jnp.sum(exponent, axis=1)
    weighted = jnp.sum(exponent * full_pred, axis=1)
    picked_exp = jnp.sum(jnp.where(row_onehot, exponent, jnp.float32(0.0)), axis=1)
    picked_pred = jnp.sum(jnp.where(row_onehot, full_pred, jnp.float32(0.0)), axis=1)
    rows_policy, rows_reward, rows_value = finish_rows(
        exponent,
        row_total,
        weighted,
        picked_exp,
        picked_pred,
        full_pred,
        row_onehot,
        my_payoff,
        my_propensity,
    )
    policy_term, reward_term = (
        lax.all_to_all(rows_policy, "acts", split_axis=1, concat_axis=0, tiled=True),
        lax.all_to_all(rows_reward, "acts", split_axis=1, concat_axis=0, tiled=True),
    )
    row_value = lax.all_gather(rows_value, "acts", axis=0, tiled=True)
    stacked = jnp.concatenate((policy_term, reward_term), axis=1)
    partial_grad = lax.dot_general(
        features, stacked, (((0,), (0,)), ((), ())), preferred_element_type=jnp.float32
    )
    summed = lax.psum(partial_grad.astype(jnp.bfloat16), "rows").astype(jnp.float32)
    return (summed[:, :act_block], summed[:, act_block:], row_value)


def solution(mesh):
    return jax.shard_map(
        on_device,
        mesh=mesh,
        in_specs=(
            P("rows", None),
            P(None, "acts"),
            P(None, "acts"),
            P("rows"),
            P("rows"),
            P("rows"),
        ),
        out_specs=(P(None, "acts"), P(None, "acts"), P("rows")),
        check_vma=False,
    )
```

profile of v0, /device:TPU:0, one launch (start us, length us, event | category | flops | bytes accessed | tf_op | source)
XLA Modules:
  0.0 315.7 jit_solution(8262830132904218718)
XLA Ops:
  7.2 0.0 copy-start
  7.2 1.2 copy-done
  8.4 10.1 %fusion.24 = f32[4096,256]{1,0:T(8,128)} fusion(bf16[4096,2048]{1,0:T(8,128)(2,1)} %param.6, bf16[2048,256]{1,0:T(8,128)(2,1)S(1)} %copy-done), kind=kOutput, calls=%fused_computation.32 | convolution fusion | flops 4294967296 | bytes 22020096 | tf_op jit(solution)/shard_map/dot_general | solution.py:28
  18.5 0.0 copy-start.1
  18.5 8.2 %all-to-all-start = ((f32[16,256,256]{2,1,0:T(8,128)}), f32[16,256,256]{2,1,0:T(8,128)}, u32[]{:S(2)}, u32[]{:S(2)}) async-start(f32[16,256,256]{2,1,0:T(8,128)} %bitcast.37), calls=%async_computation | async-start | bytes 8388608 | tf_op jit(solution)/shard_map/all_to_all | solution.py:33
  26.7 0.0 copy-done.1
  26.7 10.1 %fusion.25 = f32[4096,256]{1,0:T(8,128)} fusion(bf16[4096,2048]{1,0:T(8,128)(2,1)} %param.6, bf16[2048,256]{1,0:T(8,128)(2,1)S(1)} %copy-done.1), kind=kOutput, calls=%fused_computation.33 | convolution fusion | flops 4294967296 | bytes 22020096 | tf_op jit(solution)/shard_map/dot_general | solution.py:29
  36.8 53.2 %all-to-all-done = f32[16,256,256]{2,1,0:T(8,128)} async-done(((f32[16,256,256]{2,1,0:T(8,128)}), f32[16,256,256]{2,1,0:T(8,128)}, u32[]{:S(2)}, u32[]{:S(2)}) %all-to-all-start) | async-done | bytes 4194336 | tf_op jit(solution)/shard_map/all_to_all | solution.py:33
  89.9 4.7 %all-to-all-start.1 = ((f32[16,256,256]{2,1,0:T(8,128)}), f32[16,256,256]{2,1,0:T(8,128)}, u32[]{:S(2)}, u32[]{:S(2)}) async-start(f32[16,256,256]{2,1,0:T(8,128)} %bitcast.36), calls=%async_computation.1 | async-start | bytes 8388608 | tf_op jit(solution)/shard_map/all_to_all | solution.py:34
  94.7 0.0 all-reduce.2.cloned.1.call-start
  94.7 0.8 dynamic_slice.9
  95.5 2.5 reduce_max.9
  98.0 2.9 fusion.19
  100.9 54.2 %all-to-all-done.1 = f32[16,256,256]{2,1,0:T(8,128)} async-done(((f32[16,256,256]{2,1,0:T(8,128)}), f32[16,256,256]{2,1,0:T(8,128)}, u32[]{:S(2)}, u32[]{:S(2)}) %all-to-all-start.1) | async-done | bytes 4194336 | tf_op jit(solution)/shard_map/all_to_all | solution.py:34
  155.1 4.5 %fusion.11 = (f32[256]{0:T(256)S(1)}, f32[256]{0:T(256)S(1)}, f32[256]{0:T(256)S(1)}) fusion(f32[16,256,256]{2,1,0:T(8,128)} %all-to-all-done.1, f32[16,256,256]{2,1,0:T(8,128)} %all-to-all-done, f32[256]{0:T(256)S(1)} %reduce_max.9, s32[16,256]{1,0:T(8,128)S(1)} %multiply_add_fusion, s32[256]{0:T(256)S(1)} %dynamic_slice.9), kind=kLoop, calls=%fused_computation.18 | loop fusion | flops 8387840 | bytes 8410112 | tf_op jit(solution)/shard_map/reduce_sum | solution.py:46
  159.6 0.8 fusion.22
  160.4 4.6 %fusion.5 = (bf16[256,16,256]{2,0,1:T(8,128)(2,1)S(1)}, bf16[256,16,256]{2,0,1:T(8,128)(2,1)S(1)}) fusion(f32[16,256,256]{2,1,0:T(8,128)} %all-to-all-done.1, f32[16,256,256]{2,1,0:T(8,128)} %all-to-all-done, f32[256]{0:T(256)S(1)} %get-tuple-element.14, s32[16,256]{1,0:T(8,128)S(1)} %multiply_add_fusion, f32[256]{0:T(256)S(1)} %get-tuple-element.13, ...), kind=kLoop, calls=%fused_computation.9 | loop fusion | flops 13631488 | bytes 12605440 | tf_op jit(solution)/shard_map/convert_element_type | solution.py:18
  165.0 30.2 %all_to_all.61 = bf16[256,16,256]{2,0,1:T(8,128)(2,1)S(1)} all-to-all(bf16[256,16,256]{2,0,1:T(8,128)(2,1)S(1)} %get-tuple-element.15), channel_id=1, replica_groups=mesh['rows'=8,'acts'=16] {'acts'}, dimensions={1} | all-to-all | bytes 4194304 | tf_op jit(solution)/shard_map/all_to_all | solution.py:61
  195.2 28.1 %all_to_all.62 = bf16[256,16,256]{2,0,1:T(8,128)(2,1)S(1)} all-to-all(bf16[256,16,256]{2,0,1:T(8,128)(2,1)S(1)} %get-tuple-element.16), channel_id=1, replica_groups=mesh['rows'=8,'acts'=16] {'acts'}, dimensions={1} | all-to-all | bytes 4194304 | tf_op jit(solution)/shard_map/all_to_all | solution.py:62
  223.2 13.5 %fusion.16 = bf16[2048,512]{0,1:T(8,128)(2,1)} fusion(bf16[4096,2048]{1,0:T(8,128)(2,1)} %param.6, bf16[4096,256]{1,0:T(8,128)(2,1)S(1)} %bitcast.39, bf16[4096,256]{1,0:T(8,128)(2,1)S(1)} %bitcast.38), kind=kOutput, calls=%fused_computation.23 | convolution fusion | flops 8599371776 | bytes 23068672 | tf_op jit(solution)/shard_map/dot_general | solution.py:66
  236.7 0.0 all-reduce.2.cloned.1.call-update
  236.8 21.2 %all-gather = f32[16,1,256]{2,1,0:T(1,128)S(1)} all-gather(f32[1,1,256]{2,1,0:T(1,128)S(1)} %bitcast.41), channel_id=1, replica_groups=mesh['rows'=8,'acts'=16] {'acts'}, dimensions={0}, use_global_device_ids=true | all-gather | bytes 17408 | tf_op jit(solution)/shard_map/all_gather | solution.py:64
  257.9 42.2 %all-reduce.2.cloned.1.call-done = bf16[2048,512]{0,1:T(8,128)(2,1)} async-done(((bf16[2048,512]{0,1:T(8,128)(2,1)}), bf16[2048,512]{0,1:T(8,128)(2,1)}) %all-reduce.2.cloned.1.call-update) | async-done | bytes 2097168 | tf_op jit(solution)/shard_map/psum | solution.py:69
  300.1 3.4 %fusion.23 = (f32[2048,256]{0,1:T(8,128)S(1)}, f32[2048,256]{0,1:T(8,128)}) fusion(bf16[2048,512]{0,1:T(8,128)(2,1)} %all-reduce.2.cloned.1.call-done), kind=kLoop, calls=%fused_computation.31 | loop fusion | bytes 8388608 | tf_op jit(solution)/shard_map/slice | solution.py:70
  303.5 2.9 copy.11
  306.4 1.8 copy.12
  308.2 0.6 copy.15
  (1 shorter events, 0.0 us)
Async XLA Ops:
  7.2 1.2 copy-start
  18.5 8.2 %copy-start.1 = (bf16[2048,256]{1,0:T(8,128)(2,1)S(1)}, bf16[2048,256]{1,0:T(8,128)(2,1)}, u32[]{:S(2)}) copy-start(bf16[2048,256]{1,0:T(8,128)(2,1)} %param.8) | copy-start | bytes 3145732
  18.5 71.5 %all-to-all-start = ((f32[16,256,256]{2,1,0:T(8,128)}), f32[16,256,256]{2,1,0:T(8,128)}, u32[]{:S(2)}, u32[]{:S(2)}) async-start(f32[16,256,256]{2,1,0:T(8,128)} %bitcast.37), calls=%async_computation | async-start | bytes 8388608 | tf_op jit(solution)/shard_map/all_to_all | solution.py:33
  89.9 65.2 %all-to-all-start.1 = ((f32[16,256,256]{2,1,0:T(8,128)}), f32[16,256,256]{2,1,0:T(8,128)}, u32[]{:S(2)}, u32[]{:S(2)}) async-start(f32[16,256,256]{2,1,0:T(8,128)} %bitcast.36), calls=%async_computation.1 | async-start | bytes 8388608 | tf_op jit(solution)/shard_map/all_to_all | solution.py:34
  94.7 205.5 %all-reduce.2.cloned.1.call-start = ((), (), s32[]{:S(2)}) async-start(), calls=%async_computation.4 | async-start | bytes 4194304 | tf_op jit(solution)/shard_map/psum | solution.py:69
Sparse Core Ops, SparseCore 0:
  236.9 63.2 all-reduce.1
where the time goes:
time: 316 us
  waiting for transfers between devices  150 us (47%)
  blocking collectives  79.4 us (25%)
  matrix products  33.7 us (11%)
  other arithmetic  15.2 us (5%)
  between operations  14.1 us (4%)
  starting transfers between devices  12.9 us (4%)
  local copies, waits for them, and re-layouts  10.7 us (3%)
    all_to_all x1, waiting for transfers between devices, on_device(): lax.all_to_all(predicted, 'acts', split_axis=0, concat_axis=1, tiled=True)  54.2 us
    all_to_all x1, waiting for transfers between devices, on_device(): lax.all_to_all(scores, 'acts', split_axis=0, concat_axis=1, tiled=True)  53.2 us
    psum x1, waiting for transfers between devices, on_device(): lax.psum(partial_grad.astype(jnp.bfloat16), 'rows').astype(jnp.float32)  42.2 us
    all_to_all x1, blocking collectives, on_device(): lax.all_to_all(rows_policy, 'acts', split_axis=1, concat_axis=0, tiled=True)  30.2 us
    all_to_all x1, blocking collectives, on_device(): lax.all_to_all(rows_reward, 'acts', split_axis=1, concat_axis=0, tiled=True)  28.1 us
    all_gather x1, blocking collectives, on_device(): row_value = lax.all_gather(rows_value, 'acts', axis=0, tiled=True)  21.2 us
    dot_general x1, matrix products, on_device(): lax.dot_general(features, stacked, (((0,), (0,)), ((), ())), preferred_el...  13.5 us
    dot_general x1, matrix products, on_device(): jnp.dot(features, reward_weight, preferred_element_type=jnp.float32)  10.1 us
  transfers between devices with their start and end apart: 3, of which 3 were waited for; matrix products, arithmetic and copies ran while one was open for 5% of the time, Pallas kernels for 0%

commit v1 on v0

--- a/solution.py
+++ b/solution.py
@@ -61,7 +61,24 @@
         lax.all_to_all(rows_policy, "acts", split_axis=1, concat_axis=0, tiled=True),
         lax.all_to_all(rows_reward, "acts", split_axis=1, concat_axis=0, tiled=True),
     )
-    row_value = lax.all_gather(rows_value, "acts", axis=0, tiled=True)
+    ways, here, step = (lax.axis_size("acts"), lax.axis_index("acts"), rows_value.shape[0])
+    shape = [n * ways if d == 0 else n for d, n in enumerate(rows_value.shape)]
+    row_value = lax.dynamic_update_slice_in_dim(
+        jnp.zeros(shape, rows_value.dtype), rows_value, here * step, axis=0
+    )
+    going_up = going_down = rows_value
+    for far in range(1, ways // 2 + 1):
+        going_up = lax.ppermute(going_up, "acts", [(d, (d + 1) % ways) for d in range(ways)])
+        row_value = lax.dynamic_update_slice_in_dim(
+            row_value, going_up, (here - far) % ways * step, axis=0
+        )
+        if 2 * far < ways:
+            going_down = lax.ppermute(
+                going_down, "acts", [(d, (d - 1) % ways) for d in range(ways)]
+            )
+            row_value = lax.dynamic_update_slice_in_dim(
+                row_value, going_down, (here + far) % ways * step, axis=0
+            )
     stacked = jnp.concatenate((policy_term, reward_term), axis=1)
     partial_grad = lax.dot_general(
         features, stacked, (((0,), (0,)), ((), ())), preferred_element_type=jnp.float32

time: 316 us -> 317 us (level)
  starting transfers between devices: 12.9 us -> 50.4 us
  blocking collectives: 79.4 us -> 58.8 us
  waiting for transfers between devices: 150 us -> 130 us
    ppermute x0 -> x15, starting transfers between devices: none -> 37.5 us  [the longest x7 36.8 us: on_device(): lax.ppermute(going_down, 'acts', [(d, (d - 1) % ways) for d in range(ways)])]
    psum x1, waiting for transfers between devices: 42.2 us -> 8.25 us  [on_device(): lax.psum(partial_grad.astype(jnp.bfloat16), 'rows').astype(jnp.float32)]
    all_gather x1 -> x0, blocking collectives: 21.2 us -> none  [on_device(): row_value = lax.all_gather(rows_value, 'acts', axis=0, tiled=True)]
    ppermute x0 -> x15, waiting for transfers between devices: none -> 14.4 us  [the longest x8 14.4 us: on_device(): lax.ppermute(going_up, 'acts', [(d, (d + 1) % ways) for d in range(ways)])]
    dynamic_update_slice x0 -> x15, local copies, waits for them, and re-layouts: none -> 3.48 us  [the longest x8 1.78 us: on_device(): lax.dynamic_update_slice_in_dim(row_value, going_up, (here - far) % ways...]
    unnamed x7 -> x8, local copies, waits for them, and re-layouts: 6.52 us -> 5.92 us
  transfers between devices with their start and end apart: 3 -> 18, of which waited for: 3 -> 11; matrix products, arithmetic and copies ran while one was open for 5% -> 6% of each run, Pallas kernels for 0% -> 0%
where the time goes in v1:
time: 317 us; the launch traced here: 316 us
  waiting for transfers between devices  130 us (41%)
  blocking collectives  58.8 us (19%)
  starting transfers between devices  50.4 us (16%)
  matrix products  33.7 us (11%)
  other arithmetic  15.4 us (5%)
  between operations  14.2 us (4%)
  local copies, waits for them, and re-layouts  13.5 us (4%)
    all_to_all x1, waiting for transfers between devices, on_device(): lax.all_to_all(predicted, 'acts', split_axis=0, concat_axis=1, tiled=True)  54.3 us
    all_to_all x1, waiting for transfers between devices, on_device(): lax.all_to_all(scores, 'acts', split_axis=0, concat_axis=1, tiled=True)  53.2 us
    ppermute x7, starting transfers between devices, on_device(): lax.ppermute(going_down, 'acts', [(d, (d - 1) % ways) for d in range(ways)])  36.8 us
    all_to_all x1, blocking collectives, on_device(): lax.all_to_all(rows_policy, 'acts', split_axis=1, concat_axis=0, tiled=True)  30.2 us
    all_to_all x1, blocking collectives, on_device(): lax.all_to_all(rows_reward, 'acts', split_axis=1, concat_axis=0, tiled=True)  28.6 us
    ppermute x8, waiting for transfers between devices, on_device(): lax.ppermute(going_up, 'acts', [(d, (d + 1) % ways) for d in range(ways)])  14.4 us
    dot_general x1, matrix products, on_device(): lax.dot_general(features, stacked, (((0,), (0,)), ((), ())), preferred_el...  13.5 us
    dot_general x1, matrix products, on_device(): jnp.dot(features, reward_weight, preferred_element_type=jnp.float32)  10.1 us
  transfers between devices with their start and end apart: 18, of which 11 were waited for; matrix products, arithmetic and copies ran while one was open for 6% of the time, Pallas kernels for 0%

profile of v1, /device:TPU:0, one launch (start us, length us, event | category | flops | bytes accessed | tf_op | source)
XLA Modules:
  0.0 316.2 jit_solution(6908113027218442744)
XLA Ops:
  7.2 0.0 copy-start
  7.2 1.2 copy-done
  8.4 10.1 %fusion.24 = f32[4096,256]{1,0:T(8,128)} fusion(bf16[4096,2048]{1,0:T(8,128)(2,1)} %param.6, bf16[2048,256]{1,0:T(8,128)(2,1)S(1)} %copy-done), kind=kOutput, calls=%fused_computation.32 | convolution fusion | flops 4294967296 | bytes 22020096 | tf_op jit(solution)/shard_map/dot_general | solution.py:28
  18.5 8.2 %all-to-all-start = ((f32[16,256,256]{2,1,0:T(8,128)}), f32[16,256,256]{2,1,0:T(8,128)}, u32[]{:S(2)}, u32[]{:S(2)}) async-start(f32[16,256,256]{2,1,0:T(8,128)} %bitcast.35), calls=%async_computation | async-start | bytes 8388608 | tf_op jit(solution)/shard_map/all_to_all | solution.py:33
  26.7 10.1 %fusion.25 = f32[4096,256]{1,0:T(8,128)} fusion(bf16[4096,2048]{1,0:T(8,128)(2,1)} %param.6, bf16[2048,256]{1,0:T(8,128)(2,1)S(1)} %copy-done.2), kind=kOutput, calls=%fused_computation.33 | convolution fusion | flops 4294967296 | bytes 22020096 | tf_op jit(solution)/shard_map/dot_general | solution.py:29
  36.8 53.2 %all-to-all-done = f32[16,256,256]{2,1,0:T(8,128)} async-done(((f32[16,256,256]{2,1,0:T(8,128)}), f32[16,256,256]{2,1,0:T(8,128)}, u32[]{:S(2)}, u32[]{:S(2)}) %all-to-all-start) | async-done | bytes 4194336 | tf_op jit(solution)/shard_map/all_to_all | solution.py:33
  89.9 4.7 %all-to-all-start.1 = ((f32[16,256,256]{2,1,0:T(8,128)}), f32[16,256,256]{2,1,0:T(8,128)}, u32[]{:S(2)}, u32[]{:S(2)}) async-start(f32[16,256,256]{2,1,0:T(8,128)} %bitcast.34), calls=%async_computation.1 | async-start | bytes 8388608 | tf_op jit(solution)/shard_map/all_to_all | solution.py:34
  94.7 0.0 all-reduce.2.cloned.1.call-start
  94.7 0.8 dynamic_slice.9
  95.5 2.5 reduce_max.9
  98.0 2.9 fusion.19
  100.9 54.3 %all-to-all-done.1 = f32[16,256,256]{2,1,0:T(8,128)} async-done(((f32[16,256,256]{2,1,0:T(8,128)}), f32[16,256,256]{2,1,0:T(8,128)}, u32[]{:S(2)}, u32[]{:S(2)}) %all-to-all-start.1) | async-done | bytes 4194336 | tf_op jit(solution)/shard_map/all_to_all | solution.py:34
  155.1 4.5 %fusion.11 = (f32[256]{0:T(256)S(1)}, f32[256]{0:T(256)S(1)}, f32[256]{0:T(256)S(1)}) fusion(f32[16,256,256]{2,1,0:T(8,128)} %all-to-all-done.1, f32[16,256,256]{2,1,0:T(8,128)} %all-to-all-done, f32[256]{0:T(256)S(1)} %reduce_max.9, s32[16,256]{1,0:T(8,128)S(1)} %multiply_add_fusion, s32[256]{0:T(256)S(1)} %dynamic_slice.9), kind=kLoop, calls=%fused_computation.18 | loop fusion | flops 8387840 | bytes 8410112 | tf_op jit(solution)/shard_map/reduce_sum | solution.py:46
  159.7 0.9 fusion.22
  160.6 4.6 %fusion.5 = (bf16[256,16,256]{2,0,1:T(8,128)(2,1)S(1)}, bf16[256,16,256]{2,0,1:T(8,128)(2,1)S(1)}) fusion(f32[16,256,256]{2,1,0:T(8,128)} %all-to-all-done.1, f32[16,256,256]{2,1,0:T(8,128)} %all-to-all-done, f32[256]{0:T(256)S(1)} %get-tuple-element.12, s32[16,256]{1,0:T(8,128)S(1)} %multiply_add_fusion, f32[256]{0:T(256)S(1)} %get-tuple-element.11, ...), kind=kLoop, calls=%fused_computation.9 | loop fusion | flops 13631488 | bytes 12605440 | tf_op jit(solution)/shard_map/convert_element_type | solution.py:18
  165.1 30.2 %all_to_all.61 = bf16[256,16,256]{2,0,1:T(8,128)(2,1)S(1)} all-to-all(bf16[256,16,256]{2,0,1:T(8,128)(2,1)S(1)} %get-tuple-element.13), channel_id=1, replica_groups=mesh['rows'=8,'acts'=16] {'acts'}, dimensions={1} | all-to-all | bytes 4194304 | tf_op jit(solution)/shard_map/all_to_all | solution.py:61
  195.4 28.6 %all_to_all.62 = bf16[256,16,256]{2,0,1:T(8,128)(2,1)S(1)} all-to-all(bf16[256,16,256]{2,0,1:T(8,128)(2,1)S(1)} %get-tuple-element.14), channel_id=1, replica_groups=mesh['rows'=8,'acts'=16] {'acts'}, dimensions={1} | all-to-all | bytes 4194304 | tf_op jit(solution)/shard_map/all_to_all | solution.py:62
  223.9 13.5 %fusion.16 = bf16[2048,512]{0,1:T(8,128)(2,1)} fusion(bf16[4096,2048]{1,0:T(8,128)(2,1)} %param.6, bf16[4096,256]{1,0:T(8,128)(2,1)S(1)} %bitcast.37, bf16[4096,256]{1,0:T(8,128)(2,1)S(1)} %bitcast.36), kind=kOutput, calls=%fused_computation.23 | convolution fusion | flops 8599371776 | bytes 23068672 | tf_op jit(solution)/shard_map/dot_general | solution.py:83
  237.5 0.0 all-reduce.2.cloned.1.call-update
  237.6 0.7 collective-permute-start
  238.3 4.7 %collective-permute-start.1 = (f32[256]{0:T(256)S(1)}, f32[256]{0:T(256)S(1)}, u32[]{:S(2)}, u32[]{:S(2)}) collective-permute-start(f32[256]{0:T(256)S(1)} %get-tuple-element.10), channel_id=1, source_target_pairs={{0,15},{1,0},{2,1},{3,2},{4,3},{5,4},{6,5},{7,6},{8,7},{9,8},{10,9... | collective-permute-start | bytes 3080 | tf_op jit(solution)/shard_map/ppermute | solution.py:76
  243.0 1.5 collective-permute-done
  244.5 0.0 collective-permute-start.2
  244.6 0.0 collective-permute-done.1
  244.6 5.3 %collective-permute-start.3 = (f32[256]{0:T(256)S(1)}, f32[256]{0:T(256)S(1)}, u32[]{:S(2)}, u32[]{:S(2)}) collective-permute-start(f32[256]{0:T(256)S(1)} %collective-permute-done.1), channel_id=1, source_target_pairs={{0,15},{1,0},{2,1},{3,2},{4,3},{5,4},{6,5},{7,6},{8,7},{9,8},{10,9... | collective-permute-start | bytes 3080 | tf_op jit(solution)/shard_map/ppermute | solution.py:76
  249.9 1.5 collective-permute-done.2
  251.4 0.0 collective-permute-start.4
  251.4 0.0 collective-permute-done.3
  251.5 5.3 %collective-permute-start.5 = (f32[256]{0:T(256)S(1)}, f32[256]{0:T(256)S(1)}, u32[]{:S(2)}, u32[]{:S(2)}) collective-permute-start(f32[256]{0:T(256)S(1)} %collective-permute-done.3), channel_id=1, source_target_pairs={{0,15},{1,0},{2,1},{3,2},{4,3},{5,4},{6,5},{7,6},{8,7},{9,8},{10,9... | collective-permute-start | bytes 3080 | tf_op jit(solution)/shard_map/ppermute | solution.py:76
  256.8 1.5 collective-permute-done.4
  258.3 0.0 collective-permute-start.6
  258.3 0.0 collective-permute-done.5
  258.3 5.3 %collective-permute-start.7 = (f32[256]{0:T(256)S(1)}, f32[256]{0:T(256)S(1)}, u32[]{:S(2)}, u32[]{:S(2)}) collective-permute-start(f32[256]{0:T(256)S(1)} %collective-permute-done.5), channel_id=1, source_target_pairs={{0,15},{1,0},{2,1},{3,2},{4,3},{5,4},{6,5},{7,6},{8,7},{9,8},{10,9... | collective-permute-start | bytes 3080 | tf_op jit(solution)/shard_map/ppermute | solution.py:76
  263.7 1.5 collective-permute-done.6
  265.2 0.0 collective-permute-start.8
  265.2 0.0 collective-permute-done.7
  265.2 5.3 %collective-permute-start.9 = (f32[256]{0:T(256)S(1)}, f32[256]{0:T(256)S(1)}, u32[]{:S(2)}, u32[]{:S(2)}) collective-permute-start(f32[256]{0:T(256)S(1)} %collective-permute-done.7), channel_id=1, source_target_pairs={{0,15},{1,0},{2,1},{3,2},{4,3},{5,4},{6,5},{7,6},{8,7},{9,8},{10,9... | collective-permute-start | bytes 3080 | tf_op jit(solution)/shard_map/ppermute | solution.py:76
  270.6 1.5 collective-permute-done.8
  272.1 0.0 collective-permute-start.10
  272.1 5.3 %collective-permute-start.11 = (f32[256]{0:T(256)S(1)}, f32[256]{0:T(256)S(1)}, u32[]{:S(2)}, u32[]{:S(2)}) collective-permute-start(f32[256]{0:T(256)S(1)} %collective-permute-done.9), channel_id=1, source_target_pairs={{0,15},{1,0},{2,1},{3,2},{4,3},{5,4},{6,5},{7,6},{8,7},{9,8},{10,9... | collective-permute-start | bytes 3080 | tf_op jit(solution)/shard_map/ppermute | solution.py:76
  277.5 1.5 collective-permute-done.10
  279.0 5.3 %collective-permute-start.13 = (f32[256]{0:T(256)S(1)}, f32[256]{0:T(256)S(1)}, u32[]{:S(2)}, u32[]{:S(2)}) collective-permute-start(f32[256]{0:T(256)S(1)} %collective-permute-done.11), channel_id=1, source_target_pairs={{0,15},{1,0},{2,1},{3,2},{4,3},{5,4},{6,5},{7,6},{8,7},{9,8},{10,9... | collective-permute-start | bytes 3080 | tf_op jit(solution)/shard_map/ppermute | solution.py:76
  284.4 1.5 collective-permute-done.12
  285.9 0.0 collective-permute-start.14
  285.9 0.2 dynamic_update_slice.49
  286.1 0.2 dynamic_update_slice.50
  286.3 0.2 dynamic_update_slice.51
  286.6 0.2 dynamic_update_slice.52
  286.8 0.2 dynamic_update_slice.53
  287.0 0.2 dynamic_update_slice.54
  287.2 0.2 dynamic_update_slice.55
  287.5 0.2 dynamic_update_slice.56
  287.7 0.3 dynamic_update_slice.57
  288.0 0.3 dynamic_update_slice.58
  288.2 0.3 dynamic_update_slice.59
  288.5 0.3 dynamic_update_slice.60
  288.7 0.3 dynamic_update_slice.61
  289.0 0.3 dynamic_update_slice.62
  289.2 3.6 %collective-permute-done.14 = f32[256]{0:T(256)S(1)} collective-permute-done((f32[256]{0:T(256)S(1)}, f32[256]{0:T(256)S(1)}, u32[]{:S(2)}, u32[]{:S(2)}) %collective-permute-start.14) | collective-permute-done | bytes 1056 | tf_op jit(solution)/shard_map/ppermute | solution.py:71
  292.8 0.2 dynamic_update_slice.63
  293.0 8.3 %all-reduce.2.cloned.1.call-done = bf16[2048,512]{0,1:T(8,128)(2,1)} async-done(((bf16[2048,512]{0,1:T(8,128)(2,1)}), bf16[2048,512]{0,1:T(8,128)(2,1)}) %all-reduce.2.cloned.1.call-update) | async-done | bytes 2097168 | tf_op jit(solution)/shard_map/psum | solution.py:86
  301.2 3.4 %fusion.23 = (f32[2048,256]{0,1:T(8,128)}, f32[2048,256]{0,1:T(8,128)S(1)}) fusion(bf16[2048,512]{0,1:T(8,128)(2,1)} %all-reduce.2.cloned.1.call-done), kind=kLoop, calls=%fused_computation.31 | loop fusion | bytes 8388608 | tf_op jit(solution)/shard_map/slice | solution.py:87
  304.6 2.9 copy.10
  307.5 1.8 copy.9
  (10 shorter events, 0.0 us)
Async XLA Ops:
  7.2 1.2 copy-start
  18.5 8.2 %copy-start.2 = (bf16[2048,256]{1,0:T(8,128)(2,1)S(1)}, bf16[2048,256]{1,0:T(8,128)(2,1)}, u32[]{:S(2)}) copy-start(bf16[2048,256]{1,0:T(8,128)(2,1)} %param.8) | copy-start | bytes 3145732
  18.5 71.5 %all-to-all-start = ((f32[16,256,256]{2,1,0:T(8,128)}), f32[16,256,256]{2,1,0:T(8,128)}, u32[]{:S(2)}, u32[]{:S(2)}) async-start(f32[16,256,256]{2,1,0:T(8,128)} %bitcast.35), calls=%async_computation | async-start | bytes 8388608 | tf_op jit(solution)/shard_map/all_to_all | solution.py:33
  89.9 65.2 %all-to-all-start.1 = ((f32[16,256,256]{2,1,0:T(8,128)}), f32[16,256,256]{2,1,0:T(8,128)}, u32[]{:S(2)}, u32[]{:S(2)}) async-start(f32[16,256,256]{2,1,0:T(8,128)} %bitcast.34), calls=%async_computation.1 | async-start | bytes 8388608 | tf_op jit(solution)/shard_map/all_to_all | solution.py:34
  94.7 206.6 %all-reduce.2.cloned.1.call-start = ((), (), s32[]{:S(2)}) async-start(), calls=%async_computation.4 | async-start | bytes 4194304 | tf_op jit(solution)/shard_map/psum | solution.py:86
  237.6 7.0 %collective-permute-start = (f32[256]{0:T(256)S(1)}, f32[256]{0:T(256)S(1)}, u32[]{:S(2)}, u32[]{:S(2)}) collective-permute-start(f32[256]{0:T(256)S(1)} %get-tuple-element.10), channel_id=1, source_target_pairs={{0,1},{1,2},{2,3},{3,4},{4,5},{5,6},{6,7},{7,8},{8,9},{9,10},{10,1... | collective-permute-start | bytes 3080 | tf_op jit(solution)/shard_map/ppermute | solution.py:71
  238.3 6.3 %collective-permute-start.1 = (f32[256]{0:T(256)S(1)}, f32[256]{0:T(256)S(1)}, u32[]{:S(2)}, u32[]{:S(2)}) collective-permute-start(f32[256]{0:T(256)S(1)} %get-tuple-element.10), channel_id=1, source_target_pairs={{0,15},{1,0},{2,1},{3,2},{4,3},{5,4},{6,5},{7,6},{8,7},{9,8},{10,9... | collective-permute-start | bytes 3080 | tf_op jit(solution)/shard_map/ppermute | solution.py:76
  244.5 6.9 %collective-permute-start.2 = (f32[256]{0:T(256)S(1)}, f32[256]{0:T(256)S(1)}, u32[]{:S(2)}, u32[]{:S(2)}) collective-permute-start(f32[256]{0:T(256)S(1)} %collective-permute-done), channel_id=1, source_target_pairs={{0,1},{1,2},{2,3},{3,4},{4,5},{5,6},{6,7},{7,8},{8,9},{9,10},{10,1... | collective-permute-start | bytes 3080 | tf_op jit(solution)/shard_map/ppermute | solution.py:71
  244.6 6.9 %collective-permute-start.3 = (f32[256]{0:T(256)S(1)}, f32[256]{0:T(256)S(1)}, u32[]{:S(2)}, u32[]{:S(2)}) collective-permute-start(f32[256]{0:T(256)S(1)} %collective-permute-done.1), channel_id=1, source_target_pairs={{0,15},{1,0},{2,1},{3,2},{4,3},{5,4},{6,5},{7,6},{8,7},{9,8},{10,9... | collective-permute-start | bytes 3080 | tf_op jit(solution)/shard_map/ppermute | solution.py:76
  251.4 6.9 %collective-permute-start.4 = (f32[256]{0:T(256)S(1)}, f32[256]{0:T(256)S(1)}, u32[]{:S(2)}, u32[]{:S(2)}) collective-permute-start(f32[256]{0:T(256)S(1)} %collective-permute-done.2), channel_id=1, source_target_pairs={{0,1},{1,2},{2,3},{3,4},{4,5},{5,6},{6,7},{7,8},{8,9},{9,10},{10,1... | collective-permute-start | bytes 3080 | tf_op jit(solution)/shard_map/ppermute | solution.py:71
  251.5 6.9 %collective-permute-start.5 = (f32[256]{0:T(256)S(1)}, f32[256]{0:T(256)S(1)}, u32[]{:S(2)}, u32[]{:S(2)}) collective-permute-start(f32[256]{0:T(256)S(1)} %collective-permute-done.3), channel_id=1, source_target_pairs={{0,15},{1,0},{2,1},{3,2},{4,3},{5,4},{6,5},{7,6},{8,7},{9,8},{10,9... | collective-permute-start | bytes 3080 | tf_op jit(solution)/shard_map/ppermute | solution.py:76
  258.3 6.9 %collective-permute-start.6 = (f32[256]{0:T(256)S(1)}, f32[256]{0:T(256)S(1)}, u32[]{:S(2)}, u32[]{:S(2)}) collective-permute-start(f32[256]{0:T(256)S(1)} %collective-permute-done.4), channel_id=1, source_target_pairs={{0,1},{1,2},{2,3},{3,4},{4,5},{5,6},{6,7},{7,8},{8,9},{9,10},{10,1... | collective-permute-start | bytes 3080 | tf_op jit(solution)/shard_map/ppermute | solution.py:71
  258.3 6.9 %collective-permute-start.7 = (f32[256]{0:T(256)S(1)}, f32[256]{0:T(256)S(1)}, u32[]{:S(2)}, u32[]{:S(2)}) collective-permute-start(f32[256]{0:T(256)S(1)} %collective-permute-done.5), channel_id=1, source_target_pairs={{0,15},{1,0},{2,1},{3,2},{4,3},{5,4},{6,5},{7,6},{8,7},{9,8},{10,9... | collective-permute-start | bytes 3080 | tf_op jit(solution)/shard_map/ppermute | solution.py:76
  265.2 6.9 %collective-permute-start.8 = (f32[256]{0:T(256)S(1)}, f32[256]{0:T(256)S(1)}, u32[]{:S(2)}, u32[]{:S(2)}) collective-permute-start(f32[256]{0:T(256)S(1)} %collective-permute-done.6), channel_id=1, source_target_pairs={{0,1},{1,2},{2,3},{3,4},{4,5},{5,6},{6,7},{7,8},{8,9},{9,10},{10,1... | collective-permute-start | bytes 3080 | tf_op jit(solution)/shard_map/ppermute | solution.py:71
  265.2 6.9 %collective-permute-start.9 = (f32[256]{0:T(256)S(1)}, f32[256]{0:T(256)S(1)}, u32[]{:S(2)}, u32[]{:S(2)}) collective-permute-start(f32[256]{0:T(256)S(1)} %collective-permute-done.7), channel_id=1, source_target_pairs={{0,15},{1,0},{2,1},{3,2},{4,3},{5,4},{6,5},{7,6},{8,7},{9,8},{10,9... | collective-permute-start | bytes 3080 | tf_op jit(solution)/shard_map/ppermute | solution.py:76
  272.1 6.9 %collective-permute-start.10 = (f32[256]{0:T(256)S(1)}, f32[256]{0:T(256)S(1)}, u32[]{:S(2)}, u32[]{:S(2)}) collective-permute-start(f32[256]{0:T(256)S(1)} %collective-permute-done.8), channel_id=1, source_target_pairs={{0,1},{1,2},{2,3},{3,4},{4,5},{5,6},{6,7},{7,8},{8,9},{9,10},{10,1... | collective-permute-start | bytes 3080 | tf_op jit(solution)/shard_map/ppermute | solution.py:71
  272.1 6.9 %collective-permute-start.11 = (f32[256]{0:T(256)S(1)}, f32[256]{0:T(256)S(1)}, u32[]{:S(2)}, u32[]{:S(2)}) collective-permute-start(f32[256]{0:T(256)S(1)} %collective-permute-done.9), channel_id=1, source_target_pairs={{0,15},{1,0},{2,1},{3,2},{4,3},{5,4},{6,5},{7,6},{8,7},{9,8},{10,9... | collective-permute-start | bytes 3080 | tf_op jit(solution)/shard_map/ppermute | solution.py:76
  279.0 6.9 %collective-permute-start.12 = (f32[256]{0:T(256)S(1)}, f32[256]{0:T(256)S(1)}, u32[]{:S(2)}, u32[]{:S(2)}) collective-permute-start(f32[256]{0:T(256)S(1)} %collective-permute-done.10), channel_id=1, source_target_pairs={{0,1},{1,2},{2,3},{3,4},{4,5},{5,6},{6,7},{7,8},{8,9},{9,10},{10,1... | collective-permute-start | bytes 3080 | tf_op jit(solution)/shard_map/ppermute | solution.py:71
  279.0 9.9 %collective-permute-start.13 = (f32[256]{0:T(256)S(1)}, f32[256]{0:T(256)S(1)}, u32[]{:S(2)}, u32[]{:S(2)}) collective-permute-start(f32[256]{0:T(256)S(1)} %collective-permute-done.11), channel_id=1, source_target_pairs={{0,15},{1,0},{2,1},{3,2},{4,3},{5,4},{6,5},{7,6},{8,7},{9,8},{10,9... | collective-permute-start | bytes 3080 | tf_op jit(solution)/shard_map/ppermute | solution.py:76
  285.9 6.9 %collective-permute-start.14 = (f32[256]{0:T(256)S(1)}, f32[256]{0:T(256)S(1)}, u32[]{:S(2)}, u32[]{:S(2)}) collective-permute-start(f32[256]{0:T(256)S(1)} %collective-permute-done.12), channel_id=1, source_target_pairs={{0,1},{1,2},{2,3},{3,4},{4,5},{5,6},{6,7},{7,8},{8,9},{9,10},{10,1... | collective-permute-start | bytes 3080 | tf_op jit(solution)/shard_map/ppermute | solution.py:71
  293.0 11.6 %copy-start.1 = (f32[4096]{0:T(1024)}, f32[4096]{0:T(1024)S(1)}, u32[]{:S(2)}) copy-start(f32[4096]{0:T(1024)S(1)} %dynamic_update_slice.63) | copy-start | bytes 49156
Sparse Core Ops, SparseCore 0:
  237.6 63.6 all-reduce.1
